TPU v7x, 128 devices: a whole 4x4x4 slice. The times are simulated.
128 devices in a mesh: blk: 8 (over z, core), bfly: 16 (over y, x).
Axes of the slice: x: 4, y: 4, z: 4, core: 2. Of those that a mesh axis runs over, the one named last changes fastest.
Arguments:
- inputs: bfloat16 [8, 65536, 256], P('blk', 'bfly'), may hold values from -6 to 6
- col_basis: bfloat16 [8, 128, 512, 128], P('blk', 'bfly'), may hold values from -0.25 to 0.25
- col_factors: bfloat16 [8, 128, 3, 128, 256], P('blk', 'bfly'), may hold values from -0.375 to 0.375
- row_factors: bfloat16 [8, 128, 3, 128, 256], P('blk', 'bfly'), may hold values from -0.375 to 0.375
- row_basis: bfloat16 [8, 128, 512, 128], P('blk', 'bfly'), may hold values from -0.5 to 0.5
- contrast: float32 [65536], P('bfly'), may hold values from 0.5 to 2
- regroup: int32 [128], replicated, may hold values from 0 to 127, as said below
Outputs:
- result: bfloat16 [8, 65536, 256], P('blk', 'bfly')
- forward: bfloat16 [65536, 256], P(('bfly', 'blk'))
Inputs may be any that keep to these rules, and one draw needn't show every extreme that they name: regroup is a permutation of the nodes. Node g lies on index g // 8 of bfly before the midpoint and regroup[g] // 8 after it. No index hands more than 1 of its nodes to one index, and every index hands exactly 1 to some index. The number of nodes that index d hands to index (d + k) mod the size of bfly depends on k only.
All inputs are finite; a program needn't handle non-finite values.
Results may differ from a plain program's by a relative error of at most 0.024.
Values may be sent and summed in bfloat16 or wider, within the bound.
A program may use at most 64 MiB of HBM per device.

v0:
```python
import functools

import jax
import jax.numpy as jnp
from jax import lax
from jax.experimental import pallas as pl
from jax.experimental.pallas import tpu as pltpu
from jax.sharding import PartitionSpec as P

ITERS = 3
LEVELS = 3
NC = 4
OFFSETS = (0, 1, 2, 4)
PERIOD = 7
BF16 = jnp.bfloat16
F32 = jnp.float32


def matmul(a, b):
    return lax.dot_general(a, b, (((1,), (0,)), ((), ())), preferred_element_type=F32)


def matmul_t(a, b):
    return lax.dot_general(a, b, (((1,), (1,)), ((), ())), preferred_element_type=F32)


def pairs_of(stride, nodes):
    return [(h, h + stride) for h in range(nodes) if not h & stride]


def mix(states, pair_matrices):
    states = list(states)
    for level in range(LEVELS):
        for q, (h, p) in enumerate(pairs_of(1 << level, len(states))):
            both = jnp.concatenate([states[h], states[p]], axis=1)
            out = matmul_t(both, pair_matrices[level, q]).astype(BF16)
            rank = out.shape[1] // 2
            states[h], states[p] = out[:, :rank], out[:, rank:]
    return states


def unmix(states, pair_matrices):
    states = list(states)
    for level in reversed(range(LEVELS)):
        for q, (h, p) in enumerate(pairs_of(1 << level, len(states))):
            both = jnp.concatenate([states[h], states[p]], axis=1)
            out = matmul(both, pair_matrices[level, q]).astype(BF16)
            rank = out.shape[1] // 2
            states[h], states[p] = out[:, :rank], out[:, rank:]
    return states


def kernel(
    peers, blocks, scale,
    table, x_hbm, col_basis, col_factors, row_factors, row_basis, contrast,
    final, forward,
    x, v, u, w_col, w_row, first, held, landed,
    x1_send, x1_recv, z1_send, z1_recv, z2_send, z2_recv, x2_send, x2_recv,
    x_sem, v_sem, w_sem, own_sem, u_send_sem, u_recv_sem, send_sem, recv_sem,
):
    nodes = v.shape[0]
    rows = x1_send.shape[2]
    rank = x1_send.shape[3]
    d = lax.axis_index("bfly")
    me = lax.axis_index("blk")

    def bfly_peer(k):
        return {"bfly": lax.rem(d + k, peers)}

    def blk_peer(k):
        return {"blk": lax.rem(me + k, blocks)}

    barrier = pltpu.get_barrier_semaphore()

    @pl.loop(1, peers)
    def _(k):
        pl.semaphore_signal(barrier, inc=1, device_id=bfly_peer(k))

    @pl.loop(1, blocks)
    def _(k):
        pl.semaphore_signal(barrier, inc=1, device_id=blk_peer(k))

    @pl.loop(0, nodes)
    def _(g):
        pltpu.make_async_copy(x_hbm.at[g], x.at[g], x_sem.at[g]).start()
        pltpu.make_async_copy(col_basis.at[g], v.at[g], v_sem.at[g]).start()

    for which, (source, target) in enumerate(((col_factors, w_col), (row_factors, w_row))):
        for level in range(LEVELS):
            for q, (h, p) in enumerate(pairs_of(1 << level, nodes)):
                for node, row, own, other in ((h, 0, 0, rank), (p, rank, rank, 0)):
                    for start, column in ((0, own), (rank, other)):
                        pltpu.make_async_copy(
                            source.at[node, level, :, pl.ds(start, rank)],
                            target.at[level, q, pl.ds(row, rank), pl.ds(column, rank)],
                            w_sem.at[which],
                        ).start()
    own_basis = pltpu.make_async_copy(row_basis.at[me], u.at[0], own_sem)
    own_basis.start()

    pl.semaphore_wait(barrier, peers + blocks - 2)

    def basis_copy(k):
        target = lax.rem(me + k, blocks)
        return pltpu.make_async_remote_copy(
            src_ref=row_basis.at[target], dst_ref=u.at[blocks - k],
            send_sem=u_send_sem.at[k], recv_sem=u_recv_sem.at[blocks - k],
            device_id={"blk": target},
        )

    @pl.loop(1, blocks)
    def _(k):
        basis_copy(k).start()

    def send_bfly(which, send, recv, c):
        @pl.loop(1, peers)
        def _(k):
            pltpu.make_async_remote_copy(
                src_ref=send.at[c, k], dst_ref=recv.at[c, k],
                send_sem=send_sem.at[which, c], recv_sem=recv_sem.at[which, c],
                device_id=bfly_peer(k),
            ).start()

    def send_blk(which, send, recv, c):
        recv[c, 0] = send[c, 0]

        @pl.loop(1, blocks)
        def _(k):
            pltpu.make_async_remote_copy(
                src_ref=send.at[c, k], dst_ref=recv.at[c, blocks - k],
                send_sem=send_sem.at[which, c], recv_sem=recv_sem.at[which, c],
                device_id=blk_peer(k),
            ).start()

    def wait_all(which, send, recv, c):
        count = send.shape[1] - 1
        part = recv.at[c, pl.ds(1, count)]
        pltpu.make_async_copy(part, part, recv_sem.at[which, c]).wait()
        part = send.at[c, pl.ds(1, count)]
        pltpu.make_async_copy(part, part, send_sem.at[which, c]).wait()

    def route(which, line, states, send, recv, c):
        for i, state in enumerate(states):
            held[i] = state
        recv[c, 0] = held[table[line, 0]]
        for k in range(1, peers):
            send[c, k] = held[table[line, k]]
        send_bfly(which, send, recv, c)

    def arrived(line, recv, c):
        for k in range(peers):
            landed[k] = recv[c, k]
        return [landed[table[line, i]] for i in range(nodes)]

    @pl.loop(0, nodes)
    def _(g):
        pltpu.make_async_copy(x_hbm.at[g], x.at[g], x_sem.at[g]).wait()
        pltpu.make_async_copy(col_basis.at[g], v.at[g], v_sem.at[g]).wait()
        leaf = lax.dot_general(
            x[g], v[g], (((0,), (0,)), ((), ())), preferred_element_type=F32
        ).astype(BF16)
        for c in range(NC):
            first[c, g] = leaf[c * rows : (c + 1) * rows]

    pltpu.make_async_copy(w_col, w_col, w_sem.at[0]).wait()

    @pl.loop(0, NC)
    def _(c):
        states = mix([first[c, g] for g in range(nodes)], w_col)
        route(0, 0, states, x1_send, x1_recv, c)

    pltpu.make_async_copy(w_row, w_row, w_sem.at[1]).wait()

    def phase2(c):
        wait_all(0, x1_send, x1_recv, c)
        states = mix(arrived(1, x1_recv, c), w_row)
        for h in range(nodes):
            z1_send[c, lax.rem(h - me + blocks, blocks)] = states[h]
        send_blk(1, z1_send, z1_recv, c)

    def phase3(c):
        wait_all(1, z1_send, z1_recv, c)
        states = jnp.concatenate([z1_recv[c, j] for j in range(blocks)], axis=1)
        basis = jnp.concatenate([u[j] for j in range(blocks)], axis=1)
        weighted = (contrast[...] * (matmul_t(states, basis) * scale)).astype(BF16)
        back = matmul(weighted, basis).astype(BF16)
        for j in range(blocks):
            z2_send[c, j] = back[:, j * rank : (j + 1) * rank]
        send_blk(2, z2_send, z2_recv, c)

    def phase4(c):
        wait_all(2, z2_send, z2_recv, c)
        states = unmix(
            [z2_recv[c, lax.rem(h - me + blocks, blocks)] for h in range(nodes)], w_row
        )
        route(3, 2, states, x2_send, x2_recv, c)

    def phase5(c, t):
        wait_all(3, x2_send, x2_recv, c)
        states = unmix(arrived(3, x2_recv, c), w_col)

        @pl.when(t == ITERS - 1)
        def _():
            for i in range(nodes):
                final[i, pl.ds(pl.multiple_of(c * rows, rows), rows)] = states[i]

        @pl.when(t < ITERS - 1)
        def _():
            leaves = []
            for i in range(nodes):
                result = matmul_t(states[i], v[i]).astype(BF16)
                leaves.append(matmul(result, v[i]).astype(BF16))
            route(0, 0, mix(leaves, w_col), x1_send, x1_recv, c)

    @pl.loop(0, PERIOD * (ITERS - 1) + NC + OFFSETS[3])
    def _(step):
        def place(offset):
            u_step = step - offset
            shifted = u_step + PERIOD
            t = shifted // PERIOD - 1
            c = lax.rem(shifted, PERIOD)
            return t, c, (u_step >= 0) & (c < NC) & (t < ITERS)

        t, c, live = place(OFFSETS[0])

        @pl.when(live)
        def _():
            phase2(c)

        t, c, live = place(OFFSETS[1])

        @pl.when(live & (c == 0) & (t == 0))
        def _():
            own_basis.wait()

            @pl.loop(1, blocks)
            def _(k):
                basis_copy(k).wait_send()
                basis_copy(blocks - k).wait_recv()

        @pl.when(live)
        def _():
            phase3(c)

        t, c, live = place(OFFSETS[2])

        @pl.when(live)
        def _():
            phase4(c)

        @pl.when(live & (c == NC - 1) & (t == ITERS - 1))
        def _():
            states = jnp.concatenate(
                [
                    jnp.concatenate([z1_recv[e, j] for j in range(blocks)], axis=1)
                    for e in range(NC)
                ],
                axis=0,
            )
            basis = jnp.concatenate([u[j] for j in range(blocks)], axis=1)
            forward[...] = (matmul_t(basis, states) * scale).astype(BF16)

        t, c, live = place(OFFSETS[3])

        @pl.when(live)
        def _():
            phase5(c, t)


def expand_kernel(basis, state, out):
    out[0] = matmul_t(basis[0], state[0]).astype(BF16)


def shards(inputs, col_basis, col_factors, row_factors, row_basis, contrast, regroup):
    _, nodes, leaf, rank = col_basis.shape
    vectors = inputs.shape[-1]
    peers = lax.axis_size("bfly")
    blocks = lax.axis_size("blk")
    d = lax.axis_index("bfly")
    me = lax.axis_index("blk")
    rows = vectors // NC

    places = jnp.arange(nodes * peers, dtype=jnp.int32)
    offsets = jnp.arange(peers, dtype=jnp.int32)
    owner = regroup // nodes
    source = places // nodes
    mine = lax.dynamic_slice_in_dim(owner, d * nodes, nodes)
    local = jnp.arange(nodes, dtype=jnp.int32)
    there = lax.rem(mine - d + peers, peers)
    go = jnp.sum(jnp.where(there[None] == offsets[:, None], local[None], 0), axis=1)
    back_from = lax.rem(d - mine + peers, peers)
    arrives = regroup[None, :] == (d * nodes + local)[:, None]
    origin = jnp.sum(jnp.where(arrives, source[None, :], 0), axis=1)
    come_from = lax.rem(d - origin + peers, peers)
    back_to = lax.rem(origin - d + peers, peers)
    back_go = jnp.sum(jnp.where(back_to[None] == offsets[:, None], local[None], 0), axis=1)
    pad = jnp.zeros((peers - nodes,), jnp.int32)
    table = jnp.stack(
        [go, jnp.concatenate([come_from, pad]), back_go, jnp.concatenate([back_from, pad])]
    )
    weights = lax.dynamic_slice_in_dim(contrast, me * leaf, leaf).reshape(1, leaf)

    hbm = pl.BlockSpec(memory_space=pl.ANY)
    vmem = pl.BlockSpec(memory_space=pltpu.VMEM)
    wide = (NC, peers, rows, rank)
    narrow = (NC, blocks, rows, rank)
    final, forward = pl.pallas_call(
        functools.partial(kernel, peers, blocks, blocks ** (-0.5)),
        out_shape=(
            jax.ShapeDtypeStruct((nodes, vectors, rank), BF16),
            jax.ShapeDtypeStruct((leaf, vectors), BF16),
        ),
        in_specs=[pl.BlockSpec(memory_space=pltpu.SMEM), hbm, hbm, hbm, hbm, hbm, vmem],
        out_specs=(vmem, vmem),
        scratch_shapes=[
            pltpu.VMEM((nodes, leaf, vectors), BF16),
            pltpu.VMEM((nodes, leaf, rank), BF16),
            pltpu.VMEM((blocks, leaf, rank), BF16),
            pltpu.VMEM((LEVELS, nodes // 2, 2 * rank, 2 * rank), BF16),
            pltpu.VMEM((LEVELS, nodes // 2, 2 * rank, 2 * rank), BF16),
            pltpu.VMEM((NC, nodes, rows, rank), BF16),
            pltpu.VMEM((nodes, rows, rank), BF16),
            pltpu.VMEM((peers, rows, rank), BF16),
            pltpu.VMEM(wide, BF16),
            pltpu.VMEM(wide, BF16),
            pltpu.VMEM(narrow, BF16),
            pltpu.VMEM(narrow, BF16),
            pltpu.VMEM(narrow, BF16),
            pltpu.VMEM(narrow, BF16),
            pltpu.VMEM(wide, BF16),
            pltpu.VMEM(wide, BF16),
            pltpu.SemaphoreType.DMA((nodes,)),
            pltpu.SemaphoreType.DMA((nodes,)),
            pltpu.SemaphoreType.DMA((2,)),
            pltpu.SemaphoreType.DMA,
            pltpu.SemaphoreType.DMA((blocks,)),
            pltpu.SemaphoreType.DMA((blocks,)),
            pltpu.SemaphoreType.DMA((4, NC)),
            pltpu.SemaphoreType.DMA((4, NC)),
        ],
        compiler_params=pltpu.CompilerParams(collective_id=0, has_side_effects=True),
        name="butterfly",
    )(
        table,
        inputs.reshape(nodes, leaf, vectors),
        col_basis[0],
        col_factors[0],
        row_factors[0],
        row_basis[0],
        weights,
    )
    result = pl.pallas_call(
        expand_kernel,
        grid=(nodes,),
        out_shape=jax.ShapeDtypeStruct((nodes, leaf, vectors), BF16),
        in_specs=[
            pl.BlockSpec((1, leaf, rank), lambda g: (g, 0, 0)),
            pl.BlockSpec((1, vectors, rank), lambda g: (g, 0, 0)),
        ],
        out_specs=pl.BlockSpec((1, leaf, vectors), lambda g: (g, 0, 0)),
        name="expand",
    )(col_basis[0], final)
    return result.reshape(inputs.shape), forward


def solution(mesh):
    placed = (
        P("blk", "bfly", None),
        P("blk", "bfly", None, None),
        P("blk", "bfly", None, None, None),
        P("blk", "bfly", None, None, None),
        P("blk", "bfly", None, None),
        P("bfly"),
        P(),
    )
    return jax.shard_map(
        shards,
        mesh=mesh,
        in_specs=placed,
        out_specs=(P("blk", "bfly", None), P(("bfly", "blk"), None)),
        check_vma=False,
    )
```

profile of v0, /device:TPU:1, one launch (start us, length us, event | category | flops | bytes accessed | tf_op | source)
XLA Modules:
  0.0 117.7 jit_solution(9587352705892682674)
XLA Ops:
  0.6 0.7 and_select_fusion.1
  1.3 0.8 select_reduce_fusion.1
  2.2 0.1 compare_select_fusion.4
  2.2 0.1 select_reduce_fusion
  2.3 0.1 select_reduce_fusion.2
  2.4 0.6 pad_add_fusion.table
  3.0 1.3 %dynamic_slice.7 = f32[512]{0:T(512)} dynamic-slice(f32[4096]{0:T(1024)} %param.12, s32[]{:T(128)S(6)} %select_n.35), dynamic_slice_sizes={512} | dynamic-slice | bytes 4100 | tf_op jit(solution)/shard_map/dynamic_slice | solution.py:301
  4.3 106.3 %butterfly.1 = (bf16[8,256,128]{2,1,0:T(8,128)(2,1)}, bf16[512,256]{1,0:T(8,128)(2,1)}) custom-call(s32[4,16]{1,0:T(4,128)} %pad_add_fusion.table, bf16[8,512,256]{2,1,0:T(8,128)(2,1)} %bitcast.15, bf16[8,512,128]{2,1,0:T(8,128)(2,1)} %bitcast.13, bf16[8,3,128,256]{3,2,1,0:T(8,128)(2,1)} %bitcast.17, bf16[8,3,128,256]{3,2,1,0:T(8,128)(2,1)} %bitcast.18, ...), custom_call_target="tpu_custom_call" | custom-call | tf_op jit(solution)/shard_map/butterfly/pallas_call | solution.py:307
  110.7 0.0 copy-start
  110.7 6.3 %expand.1 = bf16[8,512,256]{2,1,0:T(8,128)(2,1)} custom-call(bf16[8,512,128]{2,1,0:T(8,128)(2,1)} %bitcast.14, bf16[8,256,128]{2,1,0:T(8,128)(2,1)} %get-tuple-element.4.state), custom_call_target="tpu_custom_call" | custom-call | tf_op jit(solution)/shard_map/expand/pallas_call | solution.py:352
  117.0 0.0 copy-done
  117.0 0.7 copy.10
  (4 shorter events, 0.0 us)
Async XLA Ops:
  110.7 6.3 %copy-start = (bf16[512,256]{1,0:T(8,128)(2,1)S(1)}, bf16[512,256]{1,0:T(8,128)(2,1)}, u32[]{:S(2)}) copy-start(bf16[512,256]{1,0:T(8,128)(2,1)} %get-tuple-element.15) | copy-start | bytes 786436
where the time goes:
time: 118 us
  Pallas kernels  113 us (96%)
  other arithmetic  2.35 us (2%)
  local copies, waits for them, and re-layouts  2.05 us (2%)
    pallas_call x1, Pallas kernels, shards(): pl.pallas_call(functools.partial(kernel, peers, blocks, blocks ** (-0.5))...  106 us
    pallas_call x1, Pallas kernels, shards(): pl.pallas_call(expand_kernel, grid=(nodes,), out_shape=jax.ShapeDtypeStru...  6.27 us

commit v1 on v0

--- a/solution.py
+++ b/solution.py
@@ -10,8 +10,8 @@
 ITERS = 3
 LEVELS = 3
 NC = 4
-OFFSETS = (0, 1, 2, 4)
-PERIOD = 7
+OFFSETS = (0, 1, 2, 3)
+PERIOD = 5
 BF16 = jnp.bfloat16
 F32 = jnp.float32
 
@@ -28,33 +28,50 @@
     return [(h, h + stride) for h in range(nodes) if not h & stride]
 
 
-def mix(states, pair_matrices):
+def mix_level(states, pair_matrices, level):
     states = list(states)
-    for level in range(LEVELS):
-        for q, (h, p) in enumerate(pairs_of(1 << level, len(states))):
-            both = jnp.concatenate([states[h], states[p]], axis=1)
-            out = matmul_t(both, pair_matrices[level, q]).astype(BF16)
-            rank = out.shape[1] // 2
-            states[h], states[p] = out[:, :rank], out[:, rank:]
+    for q, (h, p) in enumerate(pairs_of(1 << level, len(states))):
+        both = jnp.concatenate([states[h], states[p]], axis=1)
+        out = matmul_t(both, pair_matrices[level, q]).astype(BF16)
+        rank = out.shape[1] // 2
+        states[h], states[p] = out[:, :rank], out[:, rank:]
     return states
 
 
-def unmix(states, pair_matrices):
+def unmix_level(states, pair_matrices, level):
     states = list(states)
-    for level in reversed(range(LEVELS)):
-        for q, (h, p) in enumerate(pairs_of(1 << level, len(states))):
-            both = jnp.concatenate([states[h], states[p]], axis=1)
-            out = matmul(both, pair_matrices[level, q]).astype(BF16)
-            rank = out.shape[1] // 2
-            states[h], states[p] = out[:, :rank], out[:, rank:]
+    for q, (h, p) in enumerate(pairs_of(1 << level, len(states))):
+        both = jnp.concatenate([states[h], states[p]], axis=1)
+        out = matmul(both, pair_matrices[level, q]).astype(BF16)
+        rank = out.shape[1] // 2
+        states[h], states[p] = out[:, :rank], out[:, rank:]
     return states
+
+
+def mix(states, pair_matrices, first=0):
+    for level in range(first, LEVELS):
+        states = mix_level(states, pair_matrices, level)
+    return states
+
+
+def unmix(states, pair_matrices, last=0):
+    for level in reversed(range(last, LEVELS)):
+        states = unmix_level(states, pair_matrices, level)
+    return states
+
+
+def node_at(offsets, k):
+    place = jnp.int32(0)
+    for i, offset in enumerate(offsets):
+        place = jnp.where(offset == k, i, place)
+    return place
 
 
 def kernel(
     peers, blocks, scale,
-    table, x_hbm, col_basis, col_factors, row_factors, row_basis, contrast,
+    regroup, x_hbm, col_basis, col_factors, row_factors, row_basis, all_contrast,
     final, forward,
-    x, v, u, w_col, w_row, first, held, landed,
+    x, v, u, w_col, w_row, w_turn, contrast, first, held, landed, table,
     x1_send, x1_recv, z1_send, z1_recv, z2_send, z2_recv, x2_send, x2_recv,
     x_sem, v_sem, w_sem, own_sem, u_send_sem, u_recv_sem, send_sem, recv_sem,
 ):
@@ -72,31 +89,42 @@
 
     barrier = pltpu.get_barrier_semaphore()
 
-    @pl.loop(1, peers)
-    def _(k):
-        pl.semaphore_signal(barrier, inc=1, device_id=bfly_peer(k))
-
-    @pl.loop(1, blocks)
-    def _(k):
-        pl.semaphore_signal(barrier, inc=1, device_id=blk_peer(k))
-
     @pl.loop(0, nodes)
     def _(g):
         pltpu.make_async_copy(x_hbm.at[g], x.at[g], x_sem.at[g]).start()
         pltpu.make_async_copy(col_basis.at[g], v.at[g], v_sem.at[g]).start()
 
-    for which, (source, target) in enumerate(((col_factors, w_col), (row_factors, w_row))):
+    @pl.loop(1, peers)
+    def _(k):
+        pl.semaphore_signal(barrier, inc=1, device_id=bfly_peer(k))
+
+    @pl.loop(1, blocks)
+    def _(k):
+        pl.semaphore_signal(barrier, inc=1, device_id=blk_peer(k))
+
+    def load_pairs(which, source, target):
         for level in range(LEVELS):
             for q, (h, p) in enumerate(pairs_of(1 << level, nodes)):
-                for node, row, own, other in ((h, 0, 0, rank), (p, rank, rank, 0)):
-                    for start, column in ((0, own), (rank, other)):
-                        pltpu.make_async_copy(
-                            source.at[node, level, :, pl.ds(start, rank)],
-                            target.at[level, q, pl.ds(row, rank), pl.ds(column, rank)],
-                            w_sem.at[which],
-                        ).start()
+                moves = (
+                    (h, 0, 2 * rank, 0, 0), (p, 0, rank, rank, rank), (p, rank, rank, rank, 0)
+                )
+                for node, start, width, row, column in moves:
+                    pltpu.make_async_copy(
+                        source.at[node, level, :, pl.ds(start, width)],
+                        target.at[level, q, pl.ds(row, rank), pl.ds(column, width)],
+                        w_sem.at[which],
+                    ).start()
+
+    load_pairs(0, col_factors, w_col)
     own_basis = pltpu.make_async_copy(row_basis.at[me], u.at[0], own_sem)
     own_basis.start()
+
+    owners = [regroup[d * nodes + i] // nodes for i in range(nodes)]
+    there = [lax.rem(owner - d + peers, peers) for owner in owners]
+    for k in range(peers):
+        table[0, k] = node_at(there, k)
+    for i in range(nodes):
+        table[3, i] = lax.rem(d - owners[i] + peers, peers)
 
     pl.semaphore_wait(barrier, peers + blocks - 2)
 
@@ -169,6 +197,38 @@
         states = mix([first[c, g] for g in range(nodes)], w_col)
         route(0, 0, states, x1_send, x1_recv, c)
 
+    load_pairs(1, row_factors, w_row)
+
+    def seek(g, origins):
+        target = regroup[g]
+        source = g // nodes
+        hit = target // nodes == d
+        place = lax.rem(target, nodes)
+        return tuple(
+            jnp.where(hit & (place == h), source, origin) for h, origin in enumerate(origins)
+        )
+
+    origins = lax.fori_loop(0, nodes * peers, seek, (jnp.int32(0),) * nodes)
+    back_to = [lax.rem(origin - d + peers, peers) for origin in origins]
+    for k in range(peers):
+        table[2, k] = node_at(back_to, k)
+    for h in range(nodes):
+        table[1, h] = lax.rem(d - origins[h] + peers, peers)
+
+    for q, pair in enumerate(pairs_of(1, nodes)):
+        outer = w_col[0, q]
+        halves = []
+        for half, g in enumerate(pair):
+            gram = lax.dot_general(
+                v[g], v[g], (((0,), (0,)), ((), ())), preferred_element_type=F32
+            ).astype(BF16)
+            halves.append(matmul(outer[:, half * rank : (half + 1) * rank], gram).astype(BF16))
+        w_turn[q] = matmul_t(jnp.concatenate(halves, axis=1), outer).astype(BF16)
+
+    lines = contrast.shape[1] // rank
+    contrast[...] = jnp.concatenate(
+        [all_contrast[pl.ds(me * lines + i, 1)] for i in range(lines)], axis=1
+    )
     pltpu.make_async_copy(w_row, w_row, w_sem.at[1]).wait()
 
     def phase2(c):
@@ -182,7 +242,7 @@
         wait_all(1, z1_send, z1_recv, c)
         states = jnp.concatenate([z1_recv[c, j] for j in range(blocks)], axis=1)
         basis = jnp.concatenate([u[j] for j in range(blocks)], axis=1)
-        weighted = (contrast[...] * (matmul_t(states, basis) * scale)).astype(BF16)
+        weighted = (contrast[...] * scale * matmul_t(states, basis)).astype(BF16)
         back = matmul(weighted, basis).astype(BF16)
         for j in range(blocks):
             z2_send[c, j] = back[:, j * rank : (j + 1) * rank]
@@ -197,20 +257,22 @@
 
     def phase5(c, t):
         wait_all(3, x2_send, x2_recv, c)
-        states = unmix(arrived(3, x2_recv, c), w_col)
+        states = unmix(arrived(3, x2_recv, c), w_col, 1)
 
         @pl.when(t == ITERS - 1)
         def _():
+            last = unmix_level(states, w_col, 0)
             for i in range(nodes):
-                final[i, pl.ds(pl.multiple_of(c * rows, rows), rows)] = states[i]
+                final[i, pl.ds(pl.multiple_of(c * rows, rows), rows)] = last[i]
 
         @pl.when(t < ITERS - 1)
         def _():
-            leaves = []
-            for i in range(nodes):
-                result = matmul_t(states[i], v[i]).astype(BF16)
-                leaves.append(matmul(result, v[i]).astype(BF16))
-            route(0, 0, mix(leaves, w_col), x1_send, x1_recv, c)
+            turned = list(states)
+            for q, (h, p) in enumerate(pairs_of(1, nodes)):
+                both = jnp.concatenate([states[h], states[p]], axis=1)
+                out = matmul(both, w_turn[q]).astype(BF16)
+                turned[h], turned[p] = out[:, :rank], out[:, rank:]
+            route(0, 0, mix(turned, w_col, 1), x1_send, x1_recv, c)
 
     @pl.loop(0, PERIOD * (ITERS - 1) + NC + OFFSETS[3])
     def _(step):
@@ -267,8 +329,28 @@
             phase5(c, t)
 
 
-def expand_kernel(basis, state, out):
-    out[0] = matmul_t(basis[0], state[0]).astype(BF16)
+def expand_kernel(basis_hbm, state_hbm, out_hbm, basis, state, out, in_sem, out_sem):
+    nodes = basis.shape[0]
+
+    def load(g):
+        return (
+            pltpu.make_async_copy(basis_hbm.at[g], basis.at[g], in_sem.at[0, g]),
+            pltpu.make_async_copy(state_hbm.at[g], state.at[g], in_sem.at[1, g]),
+        )
+
+    def store(g):
+        return pltpu.make_async_copy(out.at[g], out_hbm.at[g], out_sem.at[g])
+
+    for g in range(nodes):
+        for copy in load(g):
+            copy.start()
+    for g in range(nodes):
+        for copy in load(g):
+            copy.wait()
+        out[g] = matmul_t(basis[g], state[g]).astype(BF16)
+        store(g).start()
+    for g in range(nodes):
+        store(g).wait()
 
 
 def shards(inputs, col_basis, col_factors, row_factors, row_basis, contrast, regroup):
@@ -276,30 +358,7 @@
     vectors = inputs.shape[-1]
     peers = lax.axis_size("bfly")
     blocks = lax.axis_size("blk")
-    d = lax.axis_index("bfly")
-    me = lax.axis_index("blk")
     rows = vectors // NC
-
-    places = jnp.arange(nodes * peers, dtype=jnp.int32)
-    offsets = jnp.arange(peers, dtype=jnp.int32)
-    owner = regroup // nodes
-    source = places // nodes
-    mine = lax.dynamic_slice_in_dim(owner, d * nodes, nodes)
-    local = jnp.arange(nodes, dtype=jnp.int32)
-    there = lax.rem(mine - d + peers, peers)
-    go = jnp.sum(jnp.where(there[None] == offsets[:, None], local[None], 0), axis=1)
-    back_from = lax.rem(d - mine + peers, peers)
-    arrives = regroup[None, :] == (d * nodes + local)[:, None]
-    origin = jnp.sum(jnp.where(arrives, source[None, :], 0), axis=1)
-    come_from = lax.rem(d - origin + peers, peers)
-    back_to = lax.rem(origin - d + peers, peers)
-    back_go = jnp.sum(jnp.where(back_to[None] == offsets[:, None], local[None], 0), axis=1)
-    pad = jnp.zeros((peers - nodes,), jnp.int32)
-    table = jnp.stack(
-        [go, jnp.concatenate([come_from, pad]), back_go, jnp.concatenate([back_from, pad])]
-    )
-    weights = lax.dynamic_slice_in_dim(contrast, me * leaf, leaf).reshape(1, leaf)
-
     hbm = pl.BlockSpec(memory_space=pl.ANY)
     vmem = pl.BlockSpec(memory_space=pltpu.VMEM)
     wide = (NC, peers, rows, rank)
@@ -318,9 +377,12 @@
             pltpu.VMEM((blocks, leaf, rank), BF16),
             pltpu.VMEM((LEVELS, nodes // 2, 2 * rank, 2 * rank), BF16),
             pltpu.VMEM((LEVELS, nodes // 2, 2 * rank, 2 * rank), BF16),
+            pltpu.VMEM((nodes // 2, 2 * rank, 2 * rank), BF16),
+            pltpu.VMEM((1, leaf), F32),
             pltpu.VMEM((NC, nodes, rows, rank), BF16),
             pltpu.VMEM((nodes, rows, rank), BF16),
             pltpu.VMEM((peers, rows, rank), BF16),
+            pltpu.SMEM((4, peers), jnp.int32),
             pltpu.VMEM(wide, BF16),
             pltpu.VMEM(wide, BF16),
             pltpu.VMEM(narrow, BF16),
@@ -341,23 +403,26 @@
         compiler_params=pltpu.CompilerParams(collective_id=0, has_side_effects=True),
         name="butterfly",
     )(
-        table,
+        regroup,
         inputs.reshape(nodes, leaf, vectors),
         col_basis[0],
         col_factors[0],
         row_factors[0],
         row_basis[0],
-        weights,
+        contrast.reshape(-1, rank),
     )
     result = pl.pallas_call(
         expand_kernel,
-        grid=(nodes,),
         out_shape=jax.ShapeDtypeStruct((nodes, leaf, vectors), BF16),
-        in_specs=[
-            pl.BlockSpec((1, leaf, rank), lambda g: (g, 0, 0)),
-            pl.BlockSpec((1, vectors, rank), lambda g: (g, 0, 0)),
+        in_specs=[hbm, hbm],
+        out_specs=hbm,
+        scratch_shapes=[
+            pltpu.VMEM((nodes, leaf, rank), BF16),
+            pltpu.VMEM((nodes, vectors, rank), BF16),
+            pltpu.VMEM((nodes, leaf, vectors), BF16),
+            pltpu.SemaphoreType.DMA((2, nodes)),
+            pltpu.SemaphoreType.DMA((nodes,)),
         ],
-        out_specs=pl.BlockSpec((1, leaf, vectors), lambda g: (g, 0, 0)),
         name="expand",
     )(col_basis[0], final)
     return result.reshape(inputs.shape), forward

time: 118 us -> 111 us (0.941)
  Pallas kernels: 113 us -> 110 us
  other arithmetic: 2.35 us -> 0 us
  local copies, waits for them, and re-layouts: 2.05 us -> 0.71 us
    pallas_call x1, Pallas kernels: 6.27 us -> 4.15 us  [shards(): pl.pallas_call(expand_kernel, out_shape=jax.ShapeDtypeStruct((nodes, leaf...]
    dynamic_slice x1 -> x0, local copies, waits for them, and re-layouts: 1.34 us -> none  [shards(): lax.dynamic_slice_in_dim(contrast, me * leaf, leaf).reshape(1, leaf)]
where the time goes in v1:
time: 111 us
  Pallas kernels  110 us (99%)
    pallas_call x1, Pallas kernels, shards(): pl.pallas_call(functools.partial(kernel, peers, blocks, blocks ** (-0.5))...  105 us
    pallas_call x1, Pallas kernels, shards(): pl.pallas_call(expand_kernel, out_shape=jax.ShapeDtypeStruct((nodes, leaf...  4.15 us

profile of v1, /device:TPU:1, one launch (start us, length us, event | category | flops | bytes accessed | tf_op | source)
XLA Modules:
  0.0 110.9 jit_solution(2774324929536090472)
XLA Ops:
  0.6 105.4 %butterfly.1 = (bf16[8,256,128]{2,1,0:T(8,128)(2,1)}, bf16[512,256]{1,0:T(8,128)(2,1)}) custom-call(s32[128]{0:T(128)} %regroup.1, bf16[8,512,256]{2,1,0:T(8,128)(2,1)} %bitcast.10, bf16[8,512,128]{2,1,0:T(8,128)(2,1)} %bitcast.7, bf16[8,3,128,256]{3,2,1,0:T(8,128)(2,1)} %bitcast.11, bf16[8,3,128,256]{3,2,1,0:T(8,128)(2,1)} %bitcast.12, ...), custom_call_target="tpu_custom_call" | custom-call | tf_op jit(solution)/shard_map/butterfly/pallas_call | solution.py:366
  106.0 0.0 copy-start
  106.0 4.2 %expand.1 = bf16[8,512,256]{2,1,0:T(8,128)(2,1)} custom-call(bf16[8,512,128]{2,1,0:T(8,128)(2,1)} %bitcast.8, bf16[8,256,128]{2,1,0:T(8,128)(2,1)} %get-tuple-element.4.state_hbm), custom_call_target="tpu_custom_call" | custom-call | tf_op jit(solution)/shard_map/expand/pallas_call | solution.py:414
  110.2 0.0 copy-done
  110.2 0.7 copy.10
Async XLA Ops:
  106.0 4.2 %copy-start = (bf16[512,256]{1,0:T(8,128)(2,1)S(1)}, bf16[512,256]{1,0:T(8,128)(2,1)}, u32[]{:S(2)}) copy-start(bf16[512,256]{1,0:T(8,128)(2,1)} %get-tuple-element.9) | copy-start | bytes 786436

commit v2 on v1

--- a/solution.py
+++ b/solution.py
@@ -7,11 +7,17 @@
 from jax.experimental.pallas import tpu as pltpu
 from jax.sharding import PartitionSpec as P
 
-ITERS = 3
 LEVELS = 3
 NC = 4
-OFFSETS = (0, 1, 2, 3)
-PERIOD = 5
+ORDER = (
+    20, 21, 22, 30, 31, 32, 40, 23, 41, 42, 50, 33, 51, 43, 20, 52,
+    21, 30, 53, 31, 40, 22, 41, 23, 32, 50, 33, 42, 43, 51, 20, 52,
+    30, 53, 21, 40, 22, 31, 23, 32, 41, 33, 42, 43, 50, 51, 52, 53,
+)
+BITS = 5
+PER_WORD = 6
+FORWARD = 20
+TURN = 24
 BF16 = jnp.bfloat16
 F32 = jnp.float32
 
@@ -65,6 +71,19 @@
     for i, offset in enumerate(offsets):
         place = jnp.where(offset == k, i, place)
     return place
+
+
+def steps():
+    codes = []
+    for i, entry in enumerate(ORDER):
+        phase, c = divmod(entry, 10)
+        if phase == 5 and TURN not in codes:
+            codes.append(TURN)
+        left = ORDER[i + 1 :].count(entry)
+        codes.append(4 * (phase - 2) + c + (4 if phase == 5 and not left else 0))
+        if phase == 4 and not any(later // 10 == 4 for later in ORDER[i + 1 :]):
+            codes.append(FORWARD)
+    return codes
 
 
 def kernel(
@@ -180,22 +199,29 @@
             landed[k] = recv[c, k]
         return [landed[table[line, i]] for i in range(nodes)]
 
-    @pl.loop(0, nodes)
-    def _(g):
-        pltpu.make_async_copy(x_hbm.at[g], x.at[g], x_sem.at[g]).wait()
-        pltpu.make_async_copy(col_basis.at[g], v.at[g], v_sem.at[g]).wait()
-        leaf = lax.dot_general(
-            x[g], v[g], (((0,), (0,)), ((), ())), preferred_element_type=F32
-        ).astype(BF16)
-        for c in range(NC):
-            first[c, g] = leaf[c * rows : (c + 1) * rows]
-
-    pltpu.make_async_copy(w_col, w_col, w_sem.at[0]).wait()
-
-    @pl.loop(0, NC)
-    def _(c):
-        states = mix([first[c, g] for g in range(nodes)], w_col)
-        route(0, 0, states, x1_send, x1_recv, c)
+    halves = 2
+    width = rows * NC // halves
+    for half in range(halves):
+
+        @pl.loop(0, nodes)
+        def _(g):
+            if half == 0:
+                pltpu.make_async_copy(x_hbm.at[g], x.at[g], x_sem.at[g]).wait()
+                pltpu.make_async_copy(col_basis.at[g], v.at[g], v_sem.at[g]).wait()
+            leaf = lax.dot_general(
+                x[g, :, half * width : (half + 1) * width], v[g],
+                (((0,), (0,)), ((), ())), preferred_element_type=F32,
+            ).astype(BF16)
+            for e in range(NC // halves):
+                first[half * (NC // halves) + e, g] = leaf[e * rows : (e + 1) * rows]
+
+        if half == 0:
+            pltpu.make_async_copy(w_col, w_col, w_sem.at[0]).wait()
+
+        @pl.loop(half * (NC // halves), (half + 1) * (NC // halves))
+        def _(c):
+            states = mix([first[c, g] for g in range(nodes)], w_col)
+            route(0, 0, states, x1_send, x1_recv, c)
 
     load_pairs(1, row_factors, w_row)
 
@@ -214,16 +240,6 @@
         table[2, k] = node_at(back_to, k)
     for h in range(nodes):
         table[1, h] = lax.rem(d - origins[h] + peers, peers)
-
-    for q, pair in enumerate(pairs_of(1, nodes)):
-        outer = w_col[0, q]
-        halves = []
-        for half, g in enumerate(pair):
-            gram = lax.dot_general(
-                v[g], v[g], (((0,), (0,)), ((), ())), preferred_element_type=F32
-            ).astype(BF16)
-            halves.append(matmul(outer[:, half * rank : (half + 1) * rank], gram).astype(BF16))
-        w_turn[q] = matmul_t(jnp.concatenate(halves, axis=1), outer).astype(BF16)
 
     lines = contrast.shape[1] // rank
     contrast[...] = jnp.concatenate(
@@ -255,17 +271,17 @@
         )
         route(3, 2, states, x2_send, x2_recv, c)
 
-    def phase5(c, t):
+    def phase5(c, final_step):
         wait_all(3, x2_send, x2_recv, c)
         states = unmix(arrived(3, x2_recv, c), w_col, 1)
 
-        @pl.when(t == ITERS - 1)
+        @pl.when(final_step)
         def _():
             last = unmix_level(states, w_col, 0)
             for i in range(nodes):
                 final[i, pl.ds(pl.multiple_of(c * rows, rows), rows)] = last[i]
 
-        @pl.when(t < ITERS - 1)
+        @pl.when(jnp.logical_not(final_step))
         def _():
             turned = list(states)
             for q, (h, p) in enumerate(pairs_of(1, nodes)):
@@ -274,24 +290,39 @@
                 turned[h], turned[p] = out[:, :rank], out[:, rank:]
             route(0, 0, mix(turned, w_col, 1), x1_send, x1_recv, c)
 
-    @pl.loop(0, PERIOD * (ITERS - 1) + NC + OFFSETS[3])
+    def turn():
+        for q, pair in enumerate(pairs_of(1, nodes)):
+            outer = w_col[0, q]
+            halves = []
+            for half, g in enumerate(pair):
+                gram = lax.dot_general(
+                    v[g], v[g], (((0,), (0,)), ((), ())), preferred_element_type=F32
+                ).astype(BF16)
+                halves.append(matmul(outer[:, half * rank : (half + 1) * rank], gram).astype(BF16))
+            w_turn[q] = matmul_t(jnp.concatenate(halves, axis=1), outer).astype(BF16)
+
+    codes = steps()
+    first_sum = next(i for i, code in enumerate(codes) if code // 4 == 1)
+    words = [
+        sum(code << (BITS * i) for i, code in enumerate(codes[start : start + PER_WORD]))
+        for start in range(0, len(codes), PER_WORD)
+    ]
+
+    @pl.loop(0, len(codes))
     def _(step):
-        def place(offset):
-            u_step = step - offset
-            shifted = u_step + PERIOD
-            t = shifted // PERIOD - 1
-            c = lax.rem(shifted, PERIOD)
-            return t, c, (u_step >= 0) & (c < NC) & (t < ITERS)
-
-        t, c, live = place(OFFSETS[0])
-
-        @pl.when(live)
+        word = jnp.int32(words[0])
+        for i, packed in enumerate(words[1:], 1):
+            word = jnp.where(step >= i * PER_WORD, packed, word)
+        shift = lax.rem(step, PER_WORD) * BITS
+        code = lax.shift_right_logical(word, shift) & ((1 << BITS) - 1)
+        kind = code // 4
+        c = lax.rem(code, 4)
+
+        @pl.when(kind == 0)
         def _():
             phase2(c)
 
-        t, c, live = place(OFFSETS[1])
-
-        @pl.when(live & (c == 0) & (t == 0))
+        @pl.when(step == first_sum)
         def _():
             own_basis.wait()
 
@@ -300,17 +331,19 @@
                 basis_copy(k).wait_send()
                 basis_copy(blocks - k).wait_recv()
 
-        @pl.when(live)
+        @pl.when(kind == 1)
         def _():
             phase3(c)
 
-        t, c, live = place(OFFSETS[2])
-
-        @pl.when(live)
+        @pl.when(kind == 2)
         def _():
             phase4(c)
 
-        @pl.when(live & (c == NC - 1) & (t == ITERS - 1))
+        @pl.when(code == TURN)
+        def _():
+            turn()
+
+        @pl.when(code == FORWARD)
         def _():
             states = jnp.concatenate(
                 [
@@ -322,14 +355,15 @@
             basis = jnp.concatenate([u[j] for j in range(blocks)], axis=1)
             forward[...] = (matmul_t(basis, states) * scale).astype(BF16)
 
-        t, c, live = place(OFFSETS[3])
-
-        @pl.when(live)
-        def _():
-            phase5(c, t)
-
-
-def expand_kernel(basis_hbm, state_hbm, out_hbm, basis, state, out, in_sem, out_sem):
+        @pl.when((kind == 3) | (kind == 4))
+        def _():
+            phase5(c, kind == 4)
+
+
+def expand_kernel(
+    basis_hbm, state_hbm, sum_hbm, out_hbm, forward_hbm,
+    basis, state, out, row_sum, in_sem, out_sem, sum_sem,
+):
     nodes = basis.shape[0]
 
     def load(g):
@@ -344,13 +378,20 @@
     for g in range(nodes):
         for copy in load(g):
             copy.start()
+    take = pltpu.make_async_copy(sum_hbm, row_sum, sum_sem.at[0])
+    give = pltpu.make_async_copy(row_sum, forward_hbm, sum_sem.at[1])
+    take.start()
     for g in range(nodes):
+        if g == nodes // 2:
+            take.wait()
+            give.start()
         for copy in load(g):
             copy.wait()
         out[g] = matmul_t(basis[g], state[g]).astype(BF16)
         store(g).start()
     for g in range(nodes):
         store(g).wait()
+    give.wait()
 
 
 def shards(inputs, col_basis, col_factors, row_factors, row_basis, contrast, regroup):
@@ -411,20 +452,25 @@
         row_basis[0],
         contrast.reshape(-1, rank),
     )
-    result = pl.pallas_call(
+    result, forward = pl.pallas_call(
         expand_kernel,
-        out_shape=jax.ShapeDtypeStruct((nodes, leaf, vectors), BF16),
-        in_specs=[hbm, hbm],
-        out_specs=hbm,
+        out_shape=(
+            jax.ShapeDtypeStruct((nodes, leaf, vectors), BF16),
+            jax.ShapeDtypeStruct((leaf, vectors), BF16),
+        ),
+        in_specs=[hbm, hbm, hbm],
+        out_specs=(hbm, hbm),
         scratch_shapes=[
             pltpu.VMEM((nodes, leaf, rank), BF16),
             pltpu.VMEM((nodes, vectors, rank), BF16),
             pltpu.VMEM((nodes, leaf, vectors), BF16),
+            pltpu.VMEM((leaf, vectors), BF16),
             pltpu.SemaphoreType.DMA((2, nodes)),
             pltpu.SemaphoreType.DMA((nodes,)),
+            pltpu.SemaphoreType.DMA((2,)),
         ],
         name="expand",
-    )(col_basis[0], final)
+    )(col_basis[0], final, forward)
     return result.reshape(inputs.shape), forward
 
 

time: 111 us -> 109 us (0.982); the launches traced: 111 us -> 108 us
  Pallas kernels: 110 us -> 107 us
    pallas_call x1, Pallas kernels: 105 us -> 103 us  [shards(): pl.pallas_call(functools.partial(kernel, peers, blocks, blocks ** (-0.5))...]
where the time goes in v2:
time: 109 us; the launch traced here: 108 us
  Pallas kernels  107 us (98%)
    pallas_call x1, Pallas kernels, shards(): pl.pallas_call(functools.partial(kernel, peers, blocks, blocks ** (-0.5))...  103 us
    pallas_call x1, Pallas kernels, shards(): pl.pallas_call(expand_kernel, out_shape=(jax.ShapeDtypeStruct((nodes, lea...  4.13 us

profile of v2, /device:TPU:1, one launch (start us, length us, event | category | flops | bytes accessed | tf_op | source)
XLA Modules:
  0.0 107.7 jit_solution(12901182089206490100)
XLA Ops:
  0.6 102.9 %butterfly.1 = (bf16[8,256,128]{2,1,0:T(8,128)(2,1)}, bf16[512,256]{1,0:T(8,128)(2,1)}) custom-call(s32[128]{0:T(128)} %regroup.1, bf16[8,512,256]{2,1,0:T(8,128)(2,1)} %bitcast.9, bf16[8,512,128]{2,1,0:T(8,128)(2,1)} %bitcast.7, bf16[8,3,128,256]{3,2,1,0:T(8,128)(2,1)} %bitcast.10, bf16[8,3,128,256]{3,2,1,0:T(8,128)(2,1)} %bitcast.11, ...), custom_call_target="tpu_custom_call" | custom-call | tf_op jit(solution)/shard_map/butterfly/pallas_call | solution.py:407
  103.5 4.1 %expand.1 = (bf16[8,512,256]{2,1,0:T(8,128)(2,1)}, bf16[512,256]{1,0:T(8,128)(2,1)}) custom-call(bf16[8,512,128]{2,1,0:T(8,128)(2,1)} %bitcast.8, bf16[8,256,128]{2,1,0:T(8,128)(2,1)} %get-tuple-element.6.state_hbm, bf16[512,256]{1,0:T(8,128)(2,1)} %get-tuple-element.7.sum_hbm), custom_call_target="tpu_custom_call" | custom-call | tf_op jit(solution)/shard_map/expand/pallas_call | solution.py:455

commit v3 on v2

--- a/solution.py
+++ b/solution.py
@@ -89,10 +89,10 @@
 def kernel(
     peers, blocks, scale,
     regroup, x_hbm, col_basis, col_factors, row_factors, row_basis, all_contrast,
-    final, forward,
-    x, v, u, w_col, w_row, w_turn, contrast, first, held, landed, table,
+    final_hbm, forward_hbm,
+    x, v, u, w_col, w_row, w_turn, contrast, first, held, landed, final, forward, table,
     x1_send, x1_recv, z1_send, z1_recv, z2_send, z2_recv, x2_send, x2_recv,
-    x_sem, v_sem, w_sem, own_sem, u_send_sem, u_recv_sem, send_sem, recv_sem,
+    x_sem, v_sem, w_sem, own_sem, u_send_sem, u_recv_sem, send_sem, recv_sem, out_sem,
 ):
     nodes = v.shape[0]
     rows = x1_send.shape[2]
@@ -226,15 +226,11 @@
     load_pairs(1, row_factors, w_row)
 
     def seek(g, origins):
-        target = regroup[g]
+        target = regroup[g] - d * nodes
         source = g // nodes
-        hit = target // nodes == d
-        place = lax.rem(target, nodes)
-        return tuple(
-            jnp.where(hit & (place == h), source, origin) for h, origin in enumerate(origins)
-        )
-
-    origins = lax.fori_loop(0, nodes * peers, seek, (jnp.int32(0),) * nodes)
+        return tuple(jnp.where(target == h, source, origin) for h, origin in enumerate(origins))
+
+    origins = lax.fori_loop(0, nodes * peers, seek, (jnp.int32(0),) * nodes, unroll=nodes)
     back_to = [lax.rem(origin - d + peers, peers) for origin in origins]
     for k in range(peers):
         table[2, k] = node_at(back_to, k)
@@ -279,7 +275,8 @@
         def _():
             last = unmix_level(states, w_col, 0)
             for i in range(nodes):
-                final[i, pl.ds(pl.multiple_of(c * rows, rows), rows)] = last[i]
+                final[c, i] = last[i]
+            give_final(c).start()
 
         @pl.when(jnp.logical_not(final_step))
         def _():
@@ -301,6 +298,11 @@
                 halves.append(matmul(outer[:, half * rank : (half + 1) * rank], gram).astype(BF16))
             w_turn[q] = matmul_t(jnp.concatenate(halves, axis=1), outer).astype(BF16)
 
+    def give_final(c):
+        span = pl.ds(pl.multiple_of(c * rows, rows), rows)
+        return pltpu.make_async_copy(final.at[c], final_hbm.at[:, span], out_sem.at[c])
+
+    give_forward = pltpu.make_async_copy(forward, forward_hbm, out_sem.at[NC])
     codes = steps()
     first_sum = next(i for i, code in enumerate(codes) if code // 4 == 1)
     words = [
@@ -354,10 +356,17 @@
             )
             basis = jnp.concatenate([u[j] for j in range(blocks)], axis=1)
             forward[...] = (matmul_t(basis, states) * scale).astype(BF16)
+            give_forward.start()
 
         @pl.when((kind == 3) | (kind == 4))
         def _():
             phase5(c, kind == 4)
+
+    give_forward.wait()
+
+    @pl.loop(0, NC)
+    def _(c):
+        give_final(c).wait()
 
 
 def expand_kernel(
@@ -411,7 +420,7 @@
             jax.ShapeDtypeStruct((leaf, vectors), BF16),
         ),
         in_specs=[pl.BlockSpec(memory_space=pltpu.SMEM), hbm, hbm, hbm, hbm, hbm, vmem],
-        out_specs=(vmem, vmem),
+        out_specs=(hbm, hbm),
         scratch_shapes=[
             pltpu.VMEM((nodes, leaf, vectors), BF16),
             pltpu.VMEM((nodes, leaf, rank), BF16),
@@ -423,6 +432,8 @@
             pltpu.VMEM((NC, nodes, rows, rank), BF16),
             pltpu.VMEM((nodes, rows, rank), BF16),
             pltpu.VMEM((peers, rows, rank), BF16),
+            pltpu.VMEM((NC, nodes, rows, rank), BF16),
+            pltpu.VMEM((leaf, vectors), BF16),
             pltpu.SMEM((4, peers), jnp.int32),
             pltpu.VMEM(wide, BF16),
             pltpu.VMEM(wide, BF16),
@@ -440,6 +451,7 @@
             pltpu.SemaphoreType.DMA((blocks,)),
             pltpu.SemaphoreType.DMA((4, NC)),
             pltpu.SemaphoreType.DMA((4, NC)),
+            pltpu.SemaphoreType.DMA((NC + 1,)),
         ],
         compiler_params=pltpu.CompilerParams(collective_id=0, has_side_effects=True),
         name="butterfly",

time: 109 us -> 110 us (level); the launches traced: 108 us -> 110 us
  Pallas kernels: 107 us -> 110 us
    pallas_call x1, Pallas kernels: 103 us -> 106 us  [shards(): pl.pallas_call(functools.partial(kernel, peers, blocks, blocks ** (-0.5))...]
where the time goes in v3:
time: 110 us
  Pallas kernels  110 us (100%)
    pallas_call x1, Pallas kernels, shards(): pl.pallas_call(functools.partial(kernel, peers, blocks, blocks ** (-0.5))...  106 us
    pallas_call x1, Pallas kernels, shards(): pl.pallas_call(expand_kernel, out_shape=(jax.ShapeDtypeStruct((nodes, lea...  4.13 us

profile of v3, /device:TPU:1, one launch (start us, length us, event | category | flops | bytes accessed | tf_op | source)
XLA Modules:
  0.0 110.3 jit_solution(12161539999707269983)
XLA Ops:
  0.6 105.5 %butterfly.1 = (bf16[8,256,128]{2,1,0:T(8,128)(2,1)}, bf16[512,256]{1,0:T(8,128)(2,1)}) custom-call(s32[128]{0:T(128)} %regroup.1, bf16[8,512,256]{2,1,0:T(8,128)(2,1)} %bitcast.9, bf16[8,512,128]{2,1,0:T(8,128)(2,1)} %bitcast.7, bf16[8,3,128,256]{3,2,1,0:T(8,128)(2,1)} %bitcast.10, bf16[8,3,128,256]{3,2,1,0:T(8,128)(2,1)} %bitcast.11, ...), custom_call_target="tpu_custom_call" | custom-call | tf_op jit(solution)/shard_map/butterfly/pallas_call | solution.py:416
  106.2 4.1 %expand.1 = (bf16[8,512,256]{2,1,0:T(8,128)(2,1)}, bf16[512,256]{1,0:T(8,128)(2,1)}) custom-call(bf16[8,512,128]{2,1,0:T(8,128)(2,1)} %bitcast.8, bf16[8,256,128]{2,1,0:T(8,128)(2,1)} %get-tuple-element.6.state_hbm, bf16[512,256]{1,0:T(8,128)(2,1)} %get-tuple-element.7.sum_hbm), custom_call_target="tpu_custom_call" | custom-call | tf_op jit(solution)/shard_map/expand/pallas_call | solution.py:467
